TPU v7x, 128 devices: a whole 4x4x4 slice. The times are simulated.
128 devices in a mesh: req: 8 (over y, core), tok: 16 (over x, z).
Axes of the slice: x: 4, y: 4, z: 4, core: 2. Of those that a mesh axis runs over, the one named last changes fastest.
Arguments:
- layer_input: bfloat16 [16384, 2048], P(('req', 'tok')), may hold values from -12 to 12
- q_in: bfloat16 [16384, 2048], P(('req', 'tok')), may hold values from -10 to 10
- k_in: bfloat16 [16384, 2048], P(('req', 'tok')), may hold values from -10 to 10
- v_in: bfloat16 [16384, 2048], P(('req', 'tok')), may hold values from -6 to 6
- segment_ids: int32 [8, 2048], P('req'), may hold values from 0 to 3, never falling along the last dimension, each value on 1 to 1024 neighbouring positions
- lambda_parts: float32 [4, 128], replicated, may hold values from -0.8 to 0.8
- out_weight: bfloat16 [2048, 2048], replicated, may hold values from -0.125 to 0.125
- ffn_gain: float32 [2048], replicated, may hold values from 0.1 to 1.9
- gate_weight: bfloat16 [2048, 5632], P(None, 'req'), may hold values from -0.125 to 0.125
- up_weight: bfloat16 [2048, 5632], P(None, 'req'), may hold values from -0.125 to 0.125
- down_weight: bfloat16 [5632, 2048], P('req'), may hold values from -0.078125 to 0.078125
- next_gain: float32 [2048], replicated, may hold values from 0.1 to 1.9
- qkv_weight: bfloat16 [2048, 6144], P(None, 'req'), may hold values from -0.125 to 0.125
- page_owner: int32 [8, 256], P('req'), may hold values from 0 to 15, as said below
- page_slot: int32 [8, 256], P('req'), may hold values from 0 to 15, as said below
Outputs:
- layer_output: bfloat16 [16384, 2048], P(('req', 'tok'))
- q_next: bfloat16 [16384, 2048], P(('req', 'tok'))
- page_cache: bfloat16 [2048, 8, 4096], P(('req', 'tok'))
Inputs may be any that keep to these rules, and one draw needn't show every extreme that they name: `segment_ids`: segment numbers never fall along a group; each of the 4 prompts of a group has 1 to 1024 tokens, one exactly 1024. `page_owner`: the 16 pages of each device name every device of its request group as owner exactly once. `page_slot`: within a request group every pair of owner and slot is named by exactly one page.
All inputs are finite; a program needn't handle non-finite values.
Results may differ from a plain program's by a relative error of at most 0.017.
Values may be sent and summed in bfloat16 or wider, within the bound.
A program may use at most 192 MiB of HBM per device.

v0:
```python
import math
import jax
import jax.numpy as jnp
from jax import lax
from jax.sharding import PartitionSpec as P

HEADS = 8
PAGE = 8
NEG_FILL = -1e30
LAMBDA_INIT = 0.2
EPSILON = 1e-05


def rms_rows(values):
    return values * lax.rsqrt(jnp.mean(values * values, axis=-1, keepdims=True) + EPSILON)


def lambda_value(lambda_parts):
    first_term = jnp.exp(jnp.sum(lambda_parts[0] * lambda_parts[1]))
    second_term = jnp.exp(jnp.sum(lambda_parts[2] * lambda_parts[3]))
    return first_term - second_term + LAMBDA_INIT


def body(
    layer_input,
    q_in,
    k_in,
    v_in,
    segment_ids,
    lambda_parts,
    out_weight,
    ffn_gain,
    gate_weight,
    up_weight,
    down_weight,
    next_gain,
    qkv_weight,
    page_owner,
    page_slot,
):
    row_count = q_in.shape[0]
    feat_width = q_in.shape[1]
    head_dim = feat_width // (2 * HEADS)
    peer_count = lax.axis_size("tok")
    tok_place = lax.axis_index("tok")
    seg_row = segment_ids[0]
    first_row = tok_place * row_count
    query_places = first_row + jnp.arange(row_count)
    query_segs = lax.dynamic_slice_in_dim(seg_row, first_row, row_count)
    lambda_mix = lambda_value(lambda_parts)
    score_scale = 1.0 / math.sqrt(head_dim)
    query_split = q_in.reshape(row_count, HEADS, 2, head_dim)
    run_max = jnp.full((HEADS, 2, row_count), NEG_FILL, jnp.float32)
    key_rows = lax.all_gather(k_in, "tok", axis=0, tiled=True)
    value_rows = lax.all_gather(v_in, "tok", axis=0, tiled=True)
    piece_len = key_rows.shape[0]
    key_split = key_rows.reshape(piece_len, HEADS, 2, head_dim)
    value_split = value_rows.reshape(piece_len, HEADS, 2 * head_dim)
    key_places = jnp.arange(piece_len)
    visible = (seg_row[None, :] == query_segs[:, None]) & (
        key_places[None, :] <= query_places[:, None]
    )
    scores = (
        jnp.einsum("qhmd,khmd->hmqk", query_split, key_split, preferred_element_type=jnp.float32)
        * score_scale
    )
    scores = jnp.where(visible, scores, NEG_FILL)
    new_max = jnp.maximum(run_max, jnp.max(scores, axis=-1))
    weights = jnp.where(visible, jnp.exp(scores - new_max[..., None]), 0.0)
    totals = jnp.sum(weights, axis=-1)
    weighted = jnp.einsum(
        "hmqk,khe->hmqe",
        weights.astype(jnp.bfloat16),
        value_split,
        preferred_element_type=jnp.float32,
    )
    run_max, totals, weighted = (new_max, totals, weighted)
    map_outputs = weighted / totals[..., None]
    difference = map_outputs[:, 0] - lambda_mix * map_outputs[:, 1]
    head_outputs = rms_rows(difference) * (1.0 - LAMBDA_INIT)
    attention = (
        jnp.transpose(head_outputs, (1, 0, 2)).reshape(row_count, feat_width).astype(jnp.bfloat16)
    )
    residual_mid = (
        layer_input.astype(jnp.float32)
        + jnp.dot(attention, out_weight, preferred_element_type=jnp.float32)
    ).astype(jnp.bfloat16)
    gathered = lax.all_gather(residual_mid, "req", axis=0, tiled=True)
    normed = (rms_rows(gathered.astype(jnp.float32)) * ffn_gain).astype(jnp.bfloat16)
    gate_proj = jnp.dot(normed, gate_weight, preferred_element_type=jnp.float32)
    up_proj = jnp.dot(normed, up_weight, preferred_element_type=jnp.float32)
    hidden = (jax.nn.silu(gate_proj) * up_proj).astype(jnp.bfloat16)
    ffn_own = lax.psum_scatter(
        jnp.dot(hidden, down_weight, preferred_element_type=jnp.float32).astype(jnp.bfloat16),
        "req",
        scatter_dimension=0,
        tiled=True,
    ).astype(jnp.float32)
    layer_output = (residual_mid.astype(jnp.float32) + ffn_own).astype(jnp.bfloat16)
    next_normed = (rms_rows(layer_output.astype(jnp.float32)) * next_gain).astype(jnp.bfloat16)
    projected_cols = jnp.dot(
        lax.all_gather(next_normed, "req", axis=0, tiled=True),
        qkv_weight,
        preferred_element_type=jnp.float32,
    ).astype(jnp.bfloat16)
    projected = lax.all_to_all(projected_cols, "req", split_axis=0, concat_axis=1, tiled=True)
    q_next = projected[:, :feat_width]
    pages_dev = row_count // PAGE
    per_owner = pages_dev // peer_count
    key_values = projected[:, feat_width:].reshape(pages_dev, PAGE, 2 * feat_width)
    owner_all = page_owner[0].reshape(peer_count, pages_dev)
    slot_all = page_slot[0].reshape(peer_count, pages_dev)
    page_numbers = jnp.arange(pages_dev, dtype=jnp.int32)
    my_owners = lax.dynamic_index_in_dim(owner_all, tok_place, 0, keepdims=False)
    send_order = jnp.argsort(my_owners * pages_dev + page_numbers)
    outgoing = key_values[send_order].reshape(peer_count, per_owner, PAGE, 2 * feat_width)
    incoming = lax.all_to_all(outgoing, "tok", split_axis=0, concat_axis=0, tiled=True)
    rank_keys = jnp.where(
        owner_all == tok_place, page_numbers[None, :], pages_dev + page_numbers[None, :]
    )
    chosen_pages = jnp.argsort(rank_keys, axis=1)[:, :per_owner]
    slot_list = jnp.take_along_axis(slot_all, chosen_pages, axis=1).reshape(pages_dev)
    page_cache = (
        jnp.zeros((pages_dev, PAGE, 2 * feat_width), jnp.bfloat16)
        .at[slot_list]
        .set(incoming.reshape(pages_dev, PAGE, 2 * feat_width))
    )
    return (layer_output, q_next, page_cache)


def solution(mesh):
    in_specs = (
        P(("req", "tok"), None),
        P(("req", "tok"), None),
        P(("req", "tok"), None),
        P(("req", "tok"), None),
        P("req", None),
        P(),
        P(),
        P(),
        P(None, "req"),
        P(None, "req"),
        P("req", None),
        P(),
        P(None, "req"),
        P("req", None),
        P("req", None),
    )
    out_specs = (P(("req", "tok"), None), P(("req", "tok"), None), P(("req", "tok"), None, None))
    return jax.shard_map(body, mesh=mesh, in_specs=in_specs, out_specs=out_specs, check_vma=False)
```

profile of v0, /device:TPU:0, one launch (start us, length us, event | category | flops | bytes accessed | tf_op | source)
XLA Modules:
  0.0 395.1 jit_solution(589856986905657744)
XLA Ops:
  7.2 0.0 copy-start
  7.2 0.0 copy-start.7
  7.2 0.0 all-gather.5.cloned.1.call-start
  7.2 2.2 copy.35
  9.4 0.0 all-gather.5.cloned.1.call-update
  9.5 0.0 all-gather.7.cloned.1.call-start
  9.5 2.0 copy.38
  11.6 0.0 all-gather.7.cloned.1.call-update
  11.6 0.0 all-gather.9.cloned.1.call-start
  11.6 2.2 reshape.96
  13.8 0.0 copy-done.7
  13.8 0.6 multiply_reduce_fusion.1
  15.8 0.4 fusion.24
  16.2 75.5 %all-gather.5.cloned.1.call-done = bf16[2048,2048]{0,1:T(8,128)(2,1)} async-done(((bf16[128,2048]{0,1:T(8,128)(2,1)}), bf16[2048,2048]{0,1:T(8,128)(2,1)}) %all-gather.5.cloned.1.call-update) | async-done | bytes 8388624 | tf_op jit(solution)/shard_map/all_gather | solution.py:54
  91.7 6.6 %fusion = (f32[8,2,128]{2,1,0:T(2,128)S(1)}, f32[8,2,128,2048]{3,2,1,0:T(8,128)S(1)}) fusion(pred[128,2048]{1,0:T(8,128)(4,1)S(1)} %fusion.24, bf16[2048,8,2,128]{0,3,2,1:T(8,128)(2,1)} %bitcast.49, bf16[128,8,2,128]{3,2,1,0:T(2,128)(2,1)} %reshape.96), kind=kOutput, calls=%fused_computation.5 | convolution fusion | flops 1086322688 | bytes 25960448 | tf_op jit(solution)/shard_map/qhmd,khmd->hmqk/dot_general | solution.py:64
  98.4 0.0 copy-start.1
  98.4 5.9 %copy-done.1 = f32[8,2,128,2048]{3,2,1,0:T(8,128)} copy-done((f32[8,2,128,2048]{3,2,1,0:T(8,128)}, f32[8,2,128,2048]{3,2,1,0:T(8,128)S(1)}, u32[]{:S(2)}) %copy-start.1) | copy-done | bytes 16777240
  104.3 5.0 %fusion.1 = f32[8,2,128]{2,1,0:T(2,128)S(1)} fusion(f32[8,2,128,2048]{3,2,1,0:T(8,128)S(1)} %get-tuple-element.12, f32[8,2,128]{2,1,0:T(2,128)S(1)} %broadcast_maximum_fusion, pred[128,2048]{1,0:T(8,128)(4,1)S(1)} %fusion.24), kind=kLoop, calls=%fused_computation.6 | loop fusion | flops 20969472 | bytes 17055744 | tf_op jit(solution)/shard_map/reduce_sum | solution.py:70
  109.3 63.0 %all-gather.7.cloned.1.call-done = bf16[2048,2048]{0,1:T(8,128)(2,1)} async-done(((bf16[128,2048]{0,1:T(8,128)(2,1)}), bf16[2048,2048]{0,1:T(8,128)(2,1)}) %all-gather.7.cloned.1.call-update) | async-done | bytes 8388624 | tf_op jit(solution)/shard_map/all_gather | solution.py:55
  172.3 12.6 %broadcast_divide_fusion = f32[8,2,128,256]{3,2,1,0:T(8,128)S(1)} fusion(f32[8,2,128]{2,1,0:T(2,128)S(1)} %fusion.1, bf16[2048,8,256,1]{0,2,3,1:T(8,128)(2,1)} %bitcast.56, f32[8,2,128,2048]{3,2,1,0:T(8,128)} %copy-done.1, f32[8,2,128]{2,1,0:T(2,128)S(1)} %broadcast_maximum_fusion, pred[128,2048]{1,0:T(8,128)(4,1)S(1)} %fusion.24), kind=kOutput, calls=%fused_computation.37 | convolution fusion | flops 2168979456 | bytes 27541504 | tf_op jit(solution)/shard_map/hmqk,khe->hmqe/dot_general | solution.py:71
  184.9 0.2 multiply_reduce_fusion
  185.1 1.1 fusion.25
  186.2 2.0 copy.40
  188.3 5.7 %fusion.13 = bf16[128,2048]{1,0:T(8,128)(2,1)} fusion(bf16[128,2048]{0,1:T(8,128)(2,1)} %bitcast.53, bf16[2048,2048]{1,0:T(8,128)(2,1)} %param.21, bf16[128,2048]{1,0:T(8,128)(2,1)} %param.15), kind=kOutput, calls=%fused_computation.22 | convolution fusion | flops 1074528256 | bytes 9961472 | tf_op jit(solution)/shard_map/dot_general | solution.py:86
  193.9 0.0 all-gather.9.cloned.1.call-update
  193.9 0.2 reduce-scatter.2.cloned.1.call-start
  194.2 31.3 %all-gather.9.cloned.1.call-done = bf16[1024,2048]{1,0:T(8,128)(2,1)} async-done(((bf16[128,2048]{1,0:T(8,128)(2,1)}), bf16[1024,2048]{1,0:T(8,128)(2,1)}) %all-gather.9.cloned.1.call-update) | async-done | bytes 4194320 | tf_op jit(solution)/shard_map/all_gather | solution.py:88
  225.5 3.2 fusion.3
  228.7 0.0 copy-done.10
  228.7 0.2 copy-done.3
  228.9 6.7 %fusion.15 = f32[1024,704]{0,1:T(8,128)} fusion(bf16[2048,704]{0,1:T(8,128)(2,1)} %param.23, bf16[1024,2048]{1,0:T(8,128)(2,1)S(1)} %copy-done.3, f32[2048]{0:T(1024)S(1)} %copy-done.10, f32[1024]{0:T(1024)S(1)} %add_rsqrt_fusion), kind=kOutput, calls=%fused_computation.26 | convolution fusion | flops 2961178624 | bytes 9973760 | tf_op jit(solution)/shard_map/dot_general | solution.py:90
  235.7 12.4 %convolution_convert_fusion = bf16[1024,2048]{1,0:T(8,128)(2,1)} fusion(bf16[704,2048]{1,0:T(8,128)(2,1)} %param.25, f32[1024,704]{0,1:T(8,128)} %fusion.15, bf16[2048,704]{0,1:T(8,128)(2,1)} %param.24, bf16[1024,2048]{1,0:T(8,128)(2,1)} %all-gather.9.cloned.1.call-done, f32[2048]{0:T(1024)S(1)} %copy-done.10, f32[1024]{0:T(1024)S(1)} %add_rsqrt_fusion), kind=kOutput, calls=%fused_computation.19 | convolution fusion | flops 5920391168 | bytes 17051648 | tf_op jit(solution)/shard_map/dot_general | solution.py:94
  248.1 0.0 reduce-scatter.2.cloned.1.call-update
  248.1 0.0 all-gather.11.cloned.1.call-start
  248.1 37.9 %reduce-scatter.2.cloned.1.call-done = bf16[128,2048]{1,0:T(8,128)(2,1)} async-done(((bf16[1024,2048]{1,0:T(8,128)(2,1)}), bf16[128,2048]{1,0:T(8,128)(2,1)}) %reduce-scatter.2.cloned.1.call-update) | async-done | bytes 524304 | tf_op jit(solution)/shard_map/reduce_scatter | solution.py:93
  286.0 1.5 fusion.19
  287.5 0.8 copy-done.4
  288.3 1.0 fusion.21
  289.2 0.0 all-gather.11.cloned.1.call-update
  289.3 0.0 copy-start.8
  289.3 0.0 copy-start.9
  289.3 31.2 %all-gather.11.cloned.1.call-done = bf16[1024,2048]{1,0:T(8,128)(2,1)} async-done(((bf16[128,2048]{1,0:T(8,128)(2,1)}), bf16[1024,2048]{1,0:T(8,128)(2,1)}) %all-gather.11.cloned.1.call-update) | async-done | bytes 4194320 | tf_op jit(solution)/shard_map/all_gather | solution.py:102
  320.4 6.8 %convolution_convert_fusion.1 = bf16[1024,768]{1,0:T(8,128)(2,1)} fusion(bf16[1024,2048]{1,0:T(8,128)(2,1)} %all-gather.11.cloned.1.call-done, bf16[2048,768]{1,0:T(8,128)(2,1)S(1)} %copy-done), kind=kOutput, calls=%fused_computation.23 | convolution fusion | flops 3222011904 | bytes 8912896 | tf_op jit(solution)/shard_map/dot_general | solution.py:101
  327.2 4.3 %all-to-all-start = ((bf16[8,128,768]{2,1,0:T(8,128)(2,1)}), bf16[8,128,768]{2,1,0:T(8,128)(2,1)}, u32[]{:S(2)}, u32[]{:S(2)}) async-start(bf16[8,128,768]{2,1,0:T(8,128)(2,1)} %bitcast.54), calls=%async_computation.1 | async-start | bytes 3145728 | tf_op jit(solution)/shard_map/all_to_all | solution.py:106
  331.5 0.5 broadcast.117
  332.0 0.7 reduce.9
  332.7 0.1 reshape_squeeze.6
  332.8 0.1 copy.42
  332.9 0.7 reduce.8
  333.5 0.1 reshape_squeeze.7
  333.6 1.2 sort.35
  334.9 18.2 %all-to-all-done = bf16[8,128,768]{2,1,0:T(8,128)(2,1)} async-done(((bf16[8,128,768]{2,1,0:T(8,128)(2,1)}), bf16[8,128,768]{2,1,0:T(8,128)(2,1)}, u32[]{:S(2)}, u32[]{:S(2)}) %all-to-all-start) | async-done | bytes 1572896 | tf_op jit(solution)/shard_map/all_to_all | solution.py:106
  353.1 1.6 copy.47
  354.7 1.1 copy-done.2
  355.8 1.0 slice_bitcast_fusion
  356.9 2.8 gather_fusion
  359.7 7.0 %all-to-all-start.1 = ((bf16[16,1,8,4096]{3,2,1,0:T(8,128)(2,1)}), bf16[16,1,8,4096]{3,2,1,0:T(8,128)(2,1)}, u32[]{:S(2)}, u32[]{:S(2)}) async-start(bf16[16,1,8,4096]{3,2,1,0:T(8,128)(2,1)} %bitcast.52), calls=%async_computation.2 | async-start | bytes 2097152 | tf_op jit(solution)/shard_map/all_to_all | solution.py:117
  366.7 0.1 iota_select_fusion
  366.8 0.7 sort.34
  367.5 0.7 gather_fusion.1
  368.2 1.9 slice.42
  370.1 14.1 %all-to-all-done.1 = bf16[16,1,8,4096]{3,2,1,0:T(8,128)(2,1)} async-done(((bf16[16,1,8,4096]{3,2,1,0:T(8,128)(2,1)}), bf16[16,1,8,4096]{3,2,1,0:T(8,128)(2,1)}, u32[]{:S(2)}, u32[]{:S(2)}) %all-to-all-start.1) | async-done | bytes 1048608 | tf_op jit(solution)/shard_map/all_to_all | solution.py:117
  384.1 1.1 broadcast_in_dim.54
  385.2 3.4 scatter_fusion
  (28 shorter events, 0.1 us)
Async XLA Ops:
  7.2 313.3 %copy-start = (bf16[2048,768]{1,0:T(8,128)(2,1)S(1)}, bf16[2048,768]{1,0:T(8,128)(2,1)}, u32[]{:S(2)}) copy-start(bf16[2048,768]{1,0:T(8,128)(2,1)} %param.27) | copy-start | bytes 9437188
  7.2 6.7 %copy-start.7 = (f32[4,128]{1,0:T(4,128)S(1)}, f32[4,128]{1,0:T(4,128)}, u32[]{:S(2)}) copy-start(f32[4,128]{1,0:T(4,128)} %param.20) | copy-start | bytes 6148
  7.2 8.6 %copy-start.6 = (s32[1,2048]{1,0:T(1,128)S(1)}, s32[1,2048]{1,0:T(1,128)}, u32[]{:S(2)}) copy-start(s32[1,2048]{1,0:T(1,128)} %param.19) | copy-start | bytes 24580
  7.2 84.5 %all-gather.5.cloned.1.call-start = ((), (), s32[]{:S(2)}) async-start(), calls=%async_computation.3 | async-start | bytes 8912896 | tf_op jit(solution)/shard_map/all_gather | solution.py:54
  9.5 162.8 %all-gather.7.cloned.1.call-start = ((), (), s32[]{:S(2)}) async-start(), calls=%async_computation.4 | async-start | bytes 8912896 | tf_op jit(solution)/shard_map/all_gather | solution.py:55
  11.6 213.9 %all-gather.9.cloned.1.call-start = ((), (), s32[]{:S(2)}) async-start(), calls=%async_computation.5 | async-start | bytes 4718592 | tf_op jit(solution)/shard_map/all_gather | solution.py:88
  98.4 5.9 %copy-start.1 = (f32[8,2,128,2048]{3,2,1,0:T(8,128)}, f32[8,2,128,2048]{3,2,1,0:T(8,128)S(1)}, u32[]{:S(2)}) copy-start(f32[8,2,128,2048]{3,2,1,0:T(8,128)S(1)} %get-tuple-element.12) | copy-start | bytes 50331652
  193.9 34.8 %copy-start.10 = (f32[2048]{0:T(1024)S(1)}, f32[2048]{0:T(1024)}, u32[]{:S(2)}) copy-start(f32[2048]{0:T(1024)} %param.22) | copy-start | bytes 24580
  193.9 92.0 %reduce-scatter.2.cloned.1.call-start = ((), (), s32[]{:S(2)}) async-start(), calls=%async_computation.6 | async-start | bytes 4718592 | tf_op jit(solution)/shard_map/reduce_scatter | solution.py:93
  225.5 3.4 copy-start.3
  248.1 40.2 %copy-start.5 = (f32[2048]{0:T(1024)S(1)}, f32[2048]{0:T(1024)}, u32[]{:S(2)}) copy-start(f32[2048]{0:T(1024)} %param.26) | copy-start | bytes 24580
  248.1 72.4 %all-gather.11.cloned.1.call-start = ((), (), s32[]{:S(2)}) async-start(), calls=%async_computation.7 | async-start | bytes 4718592 | tf_op jit(solution)/shard_map/all_gather | solution.py:102
  287.5 0.8 copy-start.4
  289.3 42.8 %copy-start.8 = (s32[1,256]{1,0:T(1,128)S(1)}, s32[1,256]{1,0:T(1,128)}, u32[]{:S(2)}) copy-start(s32[1,256]{1,0:T(1,128)} %param.28) | copy-start | bytes 3076
  289.3 43.6 %copy-start.9 = (s32[1,256]{1,0:T(1,128)S(1)}, s32[1,256]{1,0:T(1,128)}, u32[]{:S(2)}) copy-start(s32[1,256]{1,0:T(1,128)} %param.29) | copy-start | bytes 3076
  327.2 25.9 %all-to-all-start = ((bf16[8,128,768]{2,1,0:T(8,128)(2,1)}), bf16[8,128,768]{2,1,0:T(8,128)(2,1)}, u32[]{:S(2)}, u32[]{:S(2)}) async-start(bf16[8,128,768]{2,1,0:T(8,128)(2,1)} %bitcast.54), calls=%async_computation.1 | async-start | bytes 3145728 | tf_op jit(solution)/shard_map/all_to_all | solution.py:106
  354.7 1.2 copy-start.2
  359.7 24.4 %all-to-all-start.1 = ((bf16[16,1,8,4096]{3,2,1,0:T(8,128)(2,1)}), bf16[16,1,8,4096]{3,2,1,0:T(8,128)(2,1)}, u32[]{:S(2)}, u32[]{:S(2)}) async-start(bf16[16,1,8,4096]{3,2,1,0:T(8,128)(2,1)} %bitcast.52), calls=%async_computation.2 | async-start | bytes 2097152 | tf_op jit(solution)/shard_map/all_to_all | solution.py:117
Sparse Core Ops, SparseCore 0:
  10.7 80.9 all-gather.4
  94.4 77.8 all-gather.6
  194.1 31.3 all-gather.8
  248.2 37.7 reduce-scatter.1
  289.4 31.0 all-gather.10
where the time goes:
time: 396 us; the launch traced here: 395 us
  waiting for transfers between devices  271 us (68%)
  matrix products  50.8 us (13%)
  local copies, waits for them, and re-layouts  29.8 us (8%)
  other arithmetic  16.5 us (4%)
  between operations  15.3 us (4%)
  starting transfers between devices  11.7 us (3%)
    all_gather x1, waiting for transfers between devices, body(): key_rows = lax.all_gather(k_in, 'tok', axis=0, tiled=True)  75.5 us
    all_gather x1, waiting for transfers between devices, body(): value_rows = lax.all_gather(v_in, 'tok', axis=0, tiled=True)  63 us
    reduce_scatter x1, waiting for transfers between devices, body(): lax.psum_scatter(jnp.dot(hidden, down_weight, preferred_element_type=jnp....  37.9 us
    all_gather x1, waiting for transfers between devices, body(): gathered = lax.all_gather(residual_mid, 'req', axis=0, tiled=True)  31.3 us
    all_gather x1, waiting for transfers between devices, body(): lax.all_gather(next_normed, 'req', axis=0, tiled=True)  31.2 us
    all_to_all x1, waiting for transfers between devices, body(): lax.all_to_all(projected_cols, 'req', split_axis=0, concat_axis=1, tiled=...  18.2 us
    all_to_all x1, waiting for transfers between devices, body(): lax.all_to_all(outgoing, 'tok', split_axis=0, concat_axis=0, tiled=True)  14.1 us
    unnamed x26, local copies, waits for them, and re-layouts  12.8 us
  transfers between devices with their start and end apart: 7, of which 7 were waited for; matrix products, arithmetic and copies ran while one was open for 6% of the time, Pallas kernels for 0%

commit v1 on v0

--- a/solution.py
+++ b/solution.py
@@ -52,7 +52,13 @@
     query_split = q_in.reshape(row_count, HEADS, 2, head_dim)
     run_max = jnp.full((HEADS, 2, row_count), NEG_FILL, jnp.float32)
     key_rows = lax.all_gather(k_in, "tok", axis=0, tiled=True)
-    value_rows = lax.all_gather(v_in, "tok", axis=0, tiled=True)
+    k_all = lax.axis_size("tok")
+    xs_all = []
+    for q in range(v_in.ndim):
+        xs_all.append(k_all if q == 0 else 1)
+    value_rows = lax.all_to_all(
+        jnp.tile(v_in, xs_all), "tok", split_axis=0, concat_axis=0, tiled=True
+    )
     piece_len = key_rows.shape[0]
     key_split = key_rows.reshape(piece_len, HEADS, 2, head_dim)
     value_split = value_rows.reshape(piece_len, HEADS, 2 * head_dim)

time: 396 us -> 453 us (1.14)
  waiting for transfers between devices: 271 us -> 312 us
  local copies, waits for them, and re-layouts: 29.8 us -> 38.3 us
  starting transfers between devices: 11.7 us -> 19.6 us
    all_to_all x0 -> x1, waiting for transfers between devices: none -> 148 us  [body(): lax.all_to_all(jnp.tile(v_in, xs_all), 'tok', split_axis=0, concat_axis=0...]
    all_gather x1 -> x0, waiting for transfers between devices: 63 us -> none  [body(): value_rows = lax.all_gather(v_in, 'tok', axis=0, tiled=True)]
    all_gather x1, waiting for transfers between devices: 75.5 us -> 22.4 us  [body(): key_rows = lax.all_gather(k_in, 'tok', axis=0, tiled=True)]
    all_gather x1, waiting for transfers between devices: 31.3 us -> 39.5 us  [body(): gathered = lax.all_gather(residual_mid, 'req', axis=0, tiled=True)]
    all_to_all x0 -> x1, starting transfers between devices: none -> 8.14 us  [body(): lax.all_to_all(jnp.tile(v_in, xs_all), 'tok', split_axis=0, concat_axis=0...]
    another operation x0 -> x1, local copies, waits for them, and re-layouts: none -> 5.33 us  [body(): jnp.tile(v_in, xs_all)]
where the time goes in v1:
time: 453 us; the launch traced here: 452 us
  waiting for transfers between devices  312 us (69%)
  matrix products  50.5 us (11%)
  local copies, waits for them, and re-layouts  38.3 us (8%)
  starting transfers between devices  19.6 us (4%)
  other arithmetic  16.4 us (4%)
  between operations  15.3 us (3%)
    all_to_all x1, waiting for transfers between devices, body(): lax.all_to_all(jnp.tile(v_in, xs_all), 'tok', split_axis=0, concat_axis=0...  148 us
    all_gather x1, waiting for transfers between devices, body(): gathered = lax.all_gather(residual_mid, 'req', axis=0, tiled=True)  39.5 us
    reduce_scatter x1, waiting for transfers between devices, body(): lax.psum_scatter(jnp.dot(hidden, down_weight, preferred_element_type=jnp....  37.9 us
    all_gather x1, waiting for transfers between devices, body(): lax.all_gather(next_normed, 'req', axis=0, tiled=True)  31.2 us
    all_gather x1, waiting for transfers between devices, body(): key_rows = lax.all_gather(k_in, 'tok', axis=0, tiled=True)  22.4 us
    all_to_all x1, waiting for transfers between devices, body(): lax.all_to_all(projected_cols, 'req', split_axis=0, concat_axis=1, tiled=...  18.2 us
    unnamed x26, local copies, waits for them, and re-layouts  16 us
    all_to_all x1, waiting for transfers between devices, body(): lax.all_to_all(outgoing, 'tok', split_axis=0, concat_axis=0, tiled=True)  14.1 us
  transfers between devices with their start and end apart: 7, of which 7 were waited for; matrix products, arithmetic and copies ran while one was open for 6% of the time, Pallas kernels for 0%

profile of v1, /device:TPU:0, one launch (start us, length us, event | category | flops | bytes accessed | tf_op | source)
XLA Modules:
  0.0 451.9 jit_solution(3771699204791995609)
XLA Ops:
  7.2 0.0 copy-start
  7.2 0.0 all-gather.4.cloned.1.call-start
  7.2 2.2 copy.33
  9.4 0.0 all-gather.4.cloned.1.call-update
  9.4 5.3 %tile.2 = bf16[16,128,2048]{2,1,0:T(8,128)(2,1)} broadcast(bf16[128,2048]{1,0:T(8,128)(2,1)} %param.18), dimensions={1,2} | broadcast | bytes 8912896 | tf_op jit(solution)/shard_map/tile | solution.py:60
  14.8 8.1 %all-to-all-start = ((bf16[16,128,2048]{2,1,0:T(8,128)(2,1)}), bf16[16,128,2048]{2,1,0:T(8,128)(2,1)}, u32[]{:S(2)}, u32[]{:S(2)}) async-start(bf16[16,128,2048]{2,1,0:T(8,128)(2,1)} %tile.2), calls=%async_computation | async-start | bytes 16777216 | tf_op jit(solution)/shard_map/all_to_all | solution.py:59
  22.9 0.0 all-gather.6.cloned.1.call-start
  23.0 2.2 reshape.104
  25.2 0.0 copy-done.7
  25.2 0.6 multiply_reduce_fusion.1
  27.2 0.0 copy-done.6
  27.2 0.4 fusion.30
  27.7 148.5 %all-to-all-done = bf16[16,128,2048]{2,1,0:T(8,128)(2,1)} async-done(((bf16[16,128,2048]{2,1,0:T(8,128)(2,1)}), bf16[16,128,2048]{2,1,0:T(8,128)(2,1)}, u32[]{:S(2)}, u32[]{:S(2)}) %all-to-all-start) | async-done | bytes 8388640 | tf_op jit(solution)/shard_map/all_to_all | solution.py:59
  176.1 10.4 %copy.45 = bf16[256,8,8,256]{3,2,1,0:T(8,128)(2,1)} copy(bf16[256,8,8,256]{3,1,2,0:T(8,128)(2,1)} %bitcast.21) | data formatting | bytes 16777216
  186.6 22.4 %all-gather.4.cloned.1.call-done = bf16[2048,2048]{0,1:T(8,128)(2,1)} async-done(((bf16[128,2048]{0,1:T(8,128)(2,1)}), bf16[2048,2048]{0,1:T(8,128)(2,1)}) %all-gather.4.cloned.1.call-update) | async-done | bytes 8388624 | tf_op jit(solution)/shard_map/all_gather | solution.py:54
  209.0 6.6 %fusion = (f32[8,2,128]{2,1,0:T(2,128)S(1)}, f32[8,2,128,2048]{3,2,1,0:T(8,128)S(1)}) fusion(pred[128,2048]{1,0:T(8,128)(4,1)S(1)} %fusion.30, bf16[2048,8,2,128]{0,3,2,1:T(8,128)(2,1)} %bitcast.48, bf16[128,8,2,128]{3,2,1,0:T(2,128)(2,1)} %reshape.104), kind=kOutput, calls=%fused_computation.5 | convolution fusion | flops 1086322688 | bytes 25960448 | tf_op jit(solution)/shard_map/qhmd,khmd->hmqk/dot_general | solution.py:70
  215.6 0.0 copy-start.1
  215.7 5.0 %fusion.1 = f32[8,2,128]{2,1,0:T(2,128)S(1)} fusion(f32[8,2,128,2048]{3,2,1,0:T(8,128)S(1)} %get-tuple-element.12, f32[8,2,128]{2,1,0:T(2,128)S(1)} %broadcast_maximum_fusion, pred[128,2048]{1,0:T(8,128)(4,1)S(1)} %fusion.30), kind=kLoop, calls=%fused_computation.6 | loop fusion | flops 20969472 | bytes 17055744 | tf_op jit(solution)/shard_map/reduce_sum | solution.py:76
  220.7 0.7 copy-done.1
  221.4 12.3 %fusion.15 = f32[8,2,128,256]{3,2,1,0:T(8,128)S(1)} fusion(bf16[2048,8,256,1]{2,1,0,3:T(8,128)(2,1)} %bitcast.49, f32[8,2,128,2048]{3,2,1,0:T(8,128)} %copy-done.1, f32[8,2,128]{2,1,0:T(2,128)S(1)} %broadcast_maximum_fusion, pred[128,2048]{1,0:T(8,128)(4,1)S(1)} %fusion.30, f32[8,2,128]{2,1,0:T(2,128)S(1)} %fusion.1), kind=kOutput, calls=%fused_computation.25 | convolution fusion | flops 2168979456 | bytes 27541504 | tf_op jit(solution)/shard_map/hmqk,khe->hmqe/dot_general | solution.py:77
  233.7 0.2 multiply_reduce_fusion
  233.9 1.1 fusion.31
  235.0 2.0 copy.37
  237.0 5.7 %fusion.14 = bf16[128,2048]{1,0:T(8,128)(2,1)} fusion(bf16[128,2048]{0,1:T(8,128)(2,1)} %bitcast.53, bf16[2048,2048]{1,0:T(8,128)(2,1)} %param.21, bf16[128,2048]{1,0:T(8,128)(2,1)} %param.15), kind=kOutput, calls=%fused_computation.23 | convolution fusion | flops 1074528256 | bytes 9961472 | tf_op jit(solution)/shard_map/dot_general | solution.py:92
  242.7 0.0 all-gather.6.cloned.1.call-update
  242.7 0.0 reduce-scatter.2.cloned.1.call-start
  242.8 39.5 %all-gather.6.cloned.1.call-done = bf16[1024,2048]{1,0:T(8,128)(2,1)} async-done(((bf16[128,2048]{1,0:T(8,128)(2,1)}), bf16[1024,2048]{1,0:T(8,128)(2,1)}) %all-gather.6.cloned.1.call-update) | async-done | bytes 4194320 | tf_op jit(solution)/shard_map/all_gather | solution.py:94
  282.3 3.2 fusion.3
  285.5 0.0 copy-done.10
  285.5 0.2 copy-done.3
  285.7 6.7 %fusion.21 = f32[1024,704]{0,1:T(8,128)} fusion(bf16[2048,704]{0,1:T(8,128)(2,1)} %param.23, bf16[1024,2048]{1,0:T(8,128)(2,1)S(1)} %copy-done.3, f32[2048]{0:T(1024)S(1)} %copy-done.10, f32[1024]{0:T(1024)S(1)} %add_rsqrt_fusion), kind=kOutput, calls=%fused_computation.28 | convolution fusion | flops 2961178624 | bytes 9973760 | tf_op jit(solution)/shard_map/dot_general | solution.py:96
  292.4 12.4 %convolution_convert_fusion = bf16[1024,2048]{1,0:T(8,128)(2,1)} fusion(bf16[704,2048]{1,0:T(8,128)(2,1)} %param.25, f32[1024,704]{0,1:T(8,128)} %fusion.21, bf16[2048,704]{0,1:T(8,128)(2,1)} %param.24, bf16[1024,2048]{1,0:T(8,128)(2,1)} %all-gather.6.cloned.1.call-done, f32[2048]{0:T(1024)S(1)} %copy-done.10, f32[1024]{0:T(1024)S(1)} %add_rsqrt_fusion), kind=kOutput, calls=%fused_computation.20 | convolution fusion | flops 5920391168 | bytes 17051648 | tf_op jit(solution)/shard_map/dot_general | solution.py:100
  304.8 0.0 reduce-scatter.2.cloned.1.call-update
  304.9 0.0 all-gather.8.cloned.1.call-start
  304.9 37.9 %reduce-scatter.2.cloned.1.call-done = bf16[128,2048]{1,0:T(8,128)(2,1)} async-done(((bf16[1024,2048]{1,0:T(8,128)(2,1)}), bf16[128,2048]{1,0:T(8,128)(2,1)}) %reduce-scatter.2.cloned.1.call-update) | async-done | bytes 524304 | tf_op jit(solution)/shard_map/reduce_scatter | solution.py:99
  342.8 1.5 fusion.25
  344.2 0.8 copy-done.4
  345.0 1.0 fusion.27
  346.0 0.0 all-gather.8.cloned.1.call-update
  346.0 0.0 copy-start.8
  346.0 0.0 copy-start.9
  346.1 31.2 %all-gather.8.cloned.1.call-done = bf16[1024,2048]{1,0:T(8,128)(2,1)} async-done(((bf16[128,2048]{1,0:T(8,128)(2,1)}), bf16[1024,2048]{1,0:T(8,128)(2,1)}) %all-gather.8.cloned.1.call-update) | async-done | bytes 4194320 | tf_op jit(solution)/shard_map/all_gather | solution.py:108
  377.2 6.8 %convolution_convert_fusion.1 = bf16[1024,768]{1,0:T(8,128)(2,1)} fusion(bf16[1024,2048]{1,0:T(8,128)(2,1)} %all-gather.8.cloned.1.call-done, bf16[2048,768]{1,0:T(8,128)(2,1)S(1)} %copy-done), kind=kOutput, calls=%fused_computation.24 | convolution fusion | flops 3222011904 | bytes 8912896 | tf_op jit(solution)/shard_map/dot_general | solution.py:107
  384.0 4.3 all-to-all-start.1
  388.3 0.5 broadcast.120
  388.8 0.7 reduce.9
  389.5 0.1 reshape_squeeze.6
  389.5 0.1 copy.39
  389.6 0.7 reduce.8
  390.3 0.1 reshape_squeeze.7
  390.4 1.2 sort.35
  391.7 18.2 %all-to-all-done.1 = bf16[8,128,768]{2,1,0:T(8,128)(2,1)} async-done(((bf16[8,128,768]{2,1,0:T(8,128)(2,1)}), bf16[8,128,768]{2,1,0:T(8,128)(2,1)}, u32[]{:S(2)}, u32[]{:S(2)}) %all-to-all-start.1) | async-done | bytes 1572896 | tf_op jit(solution)/shard_map/all_to_all | solution.py:112
  409.9 1.6 copy.44
  411.4 1.1 copy-done.2
  412.6 1.0 slice_bitcast_fusion
  413.6 2.8 gather_fusion
  416.5 7.0 %all-to-all-start.2 = ((bf16[16,1,8,4096]{3,2,1,0:T(8,128)(2,1)}), bf16[16,1,8,4096]{3,2,1,0:T(8,128)(2,1)}, u32[]{:S(2)}, u32[]{:S(2)}) async-start(bf16[16,1,8,4096]{3,2,1,0:T(8,128)(2,1)} %bitcast.52), calls=%async_computation.3 | async-start | bytes 2097152 | tf_op jit(solution)/shard_map/all_to_all | solution.py:123
  423.5 0.1 iota_select_fusion
  423.5 0.7 sort.34
  424.3 0.7 gather_fusion.1
  424.9 1.9 slice.42
  426.8 14.1 %all-to-all-done.2 = bf16[16,1,8,4096]{3,2,1,0:T(8,128)(2,1)} async-done(((bf16[16,1,8,4096]{3,2,1,0:T(8,128)(2,1)}), bf16[16,1,8,4096]{3,2,1,0:T(8,128)(2,1)}, u32[]{:S(2)}, u32[]{:S(2)}) %all-to-all-start.2) | async-done | bytes 1048608 | tf_op jit(solution)/shard_map/all_to_all | solution.py:123
  440.9 1.1 broadcast_in_dim.54
  442.0 3.4 scatter_fusion
  (28 shorter events, 0.1 us)
Async XLA Ops:
  7.2 370.1 %copy-start = (bf16[2048,768]{1,0:T(8,128)(2,1)S(1)}, bf16[2048,768]{1,0:T(8,128)(2,1)}, u32[]{:S(2)}) copy-start(bf16[2048,768]{1,0:T(8,128)(2,1)} %param.27) | copy-start | bytes 9437188
  7.2 201.8 %all-gather.4.cloned.1.call-start = ((), (), s32[]{:S(2)}) async-start(), calls=%async_computation.4 | async-start | bytes 8912896 | tf_op jit(solution)/shard_map/all_gather | solution.py:54
  14.8 10.4 %copy-start.7 = (f32[4,128]{1,0:T(4,128)S(1)}, f32[4,128]{1,0:T(4,128)}, u32[]{:S(2)}) copy-start(f32[4,128]{1,0:T(4,128)} %param.20) | copy-start | bytes 6148
  14.8 12.4 %copy-start.6 = (s32[1,2048]{1,0:T(1,128)S(1)}, s32[1,2048]{1,0:T(1,128)}, u32[]{:S(2)}) copy-start(s32[1,2048]{1,0:T(1,128)} %param.19) | copy-start | bytes 24580
  14.8 161.4 %all-to-all-start = ((bf16[16,128,2048]{2,1,0:T(8,128)(2,1)}), bf16[16,128,2048]{2,1,0:T(8,128)(2,1)}, u32[]{:S(2)}, u32[]{:S(2)}) async-start(bf16[16,128,2048]{2,1,0:T(8,128)(2,1)} %tile.2), calls=%async_computation | async-start | bytes 16777216 | tf_op jit(solution)/shard_map/all_to_all | solution.py:59
  22.9 259.3 %all-gather.6.cloned.1.call-start = ((), (), s32[]{:S(2)}) async-start(), calls=%async_computation.5 | async-start | bytes 4718592 | tf_op jit(solution)/shard_map/all_gather | solution.py:94
  215.6 5.7 %copy-start.1 = (f32[8,2,128,2048]{3,2,1,0:T(8,128)}, f32[8,2,128,2048]{3,2,1,0:T(8,128)S(1)}, u32[]{:S(2)}) copy-start(f32[8,2,128,2048]{3,2,1,0:T(8,128)S(1)} %get-tuple-element.12) | copy-start | bytes 50331652
  242.7 42.8 %copy-start.10 = (f32[2048]{0:T(1024)S(1)}, f32[2048]{0:T(1024)}, u32[]{:S(2)}) copy-start(f32[2048]{0:T(1024)} %param.22) | copy-start | bytes 24580
  242.7 100.0 %reduce-scatter.2.cloned.1.call-start = ((), (), s32[]{:S(2)}) async-start(), calls=%async_computation.6 | async-start | bytes 4718592 | tf_op jit(solution)/shard_map/reduce_scatter | solution.py:99
  282.3 3.4 copy-start.3
  304.8 40.2 %copy-start.5 = (f32[2048]{0:T(1024)S(1)}, f32[2048]{0:T(1024)}, u32[]{:S(2)}) copy-start(f32[2048]{0:T(1024)} %param.26) | copy-start | bytes 24580
  304.9 72.4 %all-gather.8.cloned.1.call-start = ((), (), s32[]{:S(2)}) async-start(), calls=%async_computation.7 | async-start | bytes 4718592 | tf_op jit(solution)/shard_map/all_gather | solution.py:108
  344.2 0.8 copy-start.4
  346.0 42.8 %copy-start.8 = (s32[1,256]{1,0:T(1,128)S(1)}, s32[1,256]{1,0:T(1,128)}, u32[]{:S(2)}) copy-start(s32[1,256]{1,0:T(1,128)} %param.28) | copy-start | bytes 3076
  346.0 43.6 %copy-start.9 = (s32[1,256]{1,0:T(1,128)S(1)}, s32[1,256]{1,0:T(1,128)}, u32[]{:S(2)}) copy-start(s32[1,256]{1,0:T(1,128)} %param.29) | copy-start | bytes 3076
  384.0 25.9 %all-to-all-start.1 = ((bf16[8,128,768]{2,1,0:T(8,128)(2,1)}), bf16[8,128,768]{2,1,0:T(8,128)(2,1)}, u32[]{:S(2)}, u32[]{:S(2)}) async-start(bf16[8,128,768]{2,1,0:T(8,128)(2,1)} %bitcast.54), calls=%async_computation.2 | async-start | bytes 3145728 | tf_op jit(solution)/shard_map/all_to_all | solution.py:112
  411.4 1.2 copy-start.2
  416.5 24.4 %all-to-all-start.2 = ((bf16[16,1,8,4096]{3,2,1,0:T(8,128)(2,1)}), bf16[16,1,8,4096]{3,2,1,0:T(8,128)(2,1)}, u32[]{:S(2)}, u32[]{:S(2)}) async-start(bf16[16,1,8,4096]{3,2,1,0:T(8,128)(2,1)} %bitcast.52), calls=%async_computation.3 | async-start | bytes 2097152 | tf_op jit(solution)/shard_map/all_to_all | solution.py:123
Sparse Core Ops, SparseCore 0:
  10.7 198.2 all-gather.3
  242.8 39.3 all-gather.5
  305.0 37.7 reduce-scatter.1
  346.2 31.0 all-gather.7
